TPU v7x, 512 devices: a whole 4x4x16 slice. The times are simulated.
512 devices in a mesh: dp: 8 (over y, core), expert: 64 (over z, x).
Axes of the slice: x: 4, y: 4, z: 16, core: 2. Of those that a mesh axis runs over, the one named last changes fastest.
Arguments:
- tokens: bfloat16 [65536, 1024], P(('dp', 'expert')), may hold values from -6 to 6
- cotangent: bfloat16 [65536, 1024], P(('dp', 'expert')), may hold values from -6 to 6
- expert_ids: int32 [65536, 2], P(('dp', 'expert')), may hold values from 0 to 31, all different within a row; in each aligned block of 128 rows (0 to 127, 128 to 255, ...) at most 10 rows name the same one
- gates: float32 [65536, 2], P(('dp', 'expert')), may hold values from 0.25 to 1
- expert_home: int32 [32], replicated, may hold values from 0 to 31, each once
- up_weight: bfloat16 [64, 1024, 768], P('expert'), as said below
- down_weight: bfloat16 [64, 768, 1024], P('expert'), as said below
Outputs:
- layer_out: bfloat16 [65536, 1024], P(('dp', 'expert'))
- grad_tokens: bfloat16 [65536, 1024], P(('dp', 'expert'))
- grad_up: bfloat16 [64, 1024, 768], P('expert', 'dp')
- grad_down: bfloat16 [64, 768, 1024], P('expert', None, 'dp')
Inputs may be any that keep to these rules, and one draw needn't show every extreme that they name: `expert_ids`: each row names 2 different experts. Among the 128 rows of one device (aligned blocks of 128 rows) no expert is named more than 10 times, a bound that some block reaches. A permutation: expert e has copies in slots expert_home[e] and expert_home[e] + 32. `up_weight`: slots s and s + 32 hold equal weights. `down_weight`: slots s and s + 32 hold equal weights.
All inputs are finite; a program needn't handle non-finite values.
Results may differ from a plain program's by a relative error of at most 0.015.
Values may be sent and summed in bfloat16 or wider, within the bound.
A program may use at most 64 MiB of HBM per device.

v0:
```python
import jax
import jax.numpy as jnp
from jax import lax
from jax.sharding import PartitionSpec as P


def shifted(value, axis, steps):
    count = lax.axis_size(axis)
    pairs = [(source, (source + steps) % count) for source in range(count)]
    return lax.ppermute(value, axis, pairs)


def silu_grad(hidden_in):
    sigmoid = jax.nn.sigmoid(hidden_in)
    return sigmoid * (1.0 + hidden_in * (1.0 - sigmoid))


def weight_terms(in_rows, pre_grad, activated, dy_rows):
    contract = (((0,), (0,)), ((), ()))
    part_up = lax.dot_general(in_rows, pre_grad, contract, preferred_element_type=jnp.float32)
    part_down = lax.dot_general(activated, dy_rows, contract, preferred_element_type=jnp.float32)
    return (part_up, part_down)


def local(tokens, cotangent, expert_ids, gates, expert_home, up_weight, down_weight):
    axis_width = lax.axis_size("expert")
    half_axis = axis_width // 2
    my_index = lax.axis_index("expert")
    token_count, model_width = tokens.shape
    top_count = expert_ids.shape[1]
    expert_count = expert_home.shape[0]
    capacity = 5 * token_count * top_count // (4 * expert_count)
    pair_expert = expert_ids.reshape(-1)
    one_hot = (pair_expert[:, None] == jnp.arange(expert_count, dtype=jnp.int32)[None, :]).astype(
        jnp.int32
    )
    ranking = jnp.sum(jnp.cumsum(one_hot, axis=0) * one_hot, axis=1) - 1
    home_device = jnp.sum(one_hot * expert_home[None, :], axis=1)
    replica = jnp.zeros_like(ranking) + my_index % 2
    target = home_device + replica * half_axis
    buffer_slot = target * capacity + ranking
    pair_number = jnp.arange(pair_expert.shape[0], dtype=jnp.int32)
    filler = jnp.zeros((axis_width * capacity,), jnp.int32).at[buffer_slot].set(pair_number + 1)
    filled = filler > 0
    source_pair = jnp.maximum(filler - 1, 0)
    source_token = source_pair // top_count
    send_rows = jnp.where(filled[:, None], tokens[source_token], jnp.zeros((), jnp.bfloat16))
    send_gate = jnp.where(filled, gates.reshape(-1)[source_pair], 0.0)
    send_cot = (send_gate[:, None] * cotangent[source_token].astype(jnp.float32)).astype(
        jnp.bfloat16
    )
    block_shape = (axis_width, capacity, model_width)
    recv_rows, recv_cot = (
        lax.all_to_all(
            send_rows.reshape(block_shape), "expert", split_axis=0, concat_axis=0, tiled=True
        ),
        lax.all_to_all(
            send_cot.reshape(block_shape), "expert", split_axis=0, concat_axis=0, tiled=True
        ),
    )
    in_rows = recv_rows.reshape(axis_width * capacity, model_width)
    dy_rows = recv_cot.reshape(axis_width * capacity, model_width)
    weight_up = up_weight[0]
    weight_down = down_weight[0]
    transposed = (((1,), (1,)), ((), ()))
    hidden_in = jnp.dot(in_rows, weight_up, preferred_element_type=jnp.float32)
    activated = jax.nn.silu(hidden_in).astype(jnp.bfloat16)
    expert_out = jnp.dot(activated, weight_down, preferred_element_type=jnp.float32).astype(
        jnp.bfloat16
    )
    act_grad = lax.dot_general(dy_rows, weight_down, transposed, preferred_element_type=jnp.float32)
    pre_grad = (act_grad * silu_grad(hidden_in)).astype(jnp.bfloat16)
    row_grad = lax.dot_general(
        pre_grad, weight_up, transposed, preferred_element_type=jnp.float32
    ).astype(jnp.bfloat16)
    back_out, back_grad = (
        lax.all_to_all(
            expert_out.reshape(block_shape), "expert", split_axis=0, concat_axis=0, tiled=True
        ),
        lax.all_to_all(
            row_grad.reshape(block_shape), "expert", split_axis=0, concat_axis=0, tiled=True
        ),
    )
    pair_out = back_out.reshape(axis_width * capacity, model_width)[buffer_slot]
    pair_grad = back_grad.reshape(axis_width * capacity, model_width)[buffer_slot]
    weighted = gates[:, :, None] * pair_out.reshape(token_count, top_count, model_width).astype(
        jnp.float32
    )
    layer_out = jnp.sum(weighted, axis=1).astype(jnp.bfloat16)
    grad_tokens = jnp.sum(
        pair_grad.reshape(token_count, top_count, model_width).astype(jnp.float32), axis=1
    ).astype(jnp.bfloat16)
    local_up, local_down = weight_terms(in_rows, pre_grad, activated, dy_rows)
    far_up, far_down = (
        shifted(local_up.astype(jnp.bfloat16), "expert", half_axis).astype(local_up.dtype),
        shifted(local_down.astype(jnp.bfloat16), "expert", half_axis).astype(local_down.dtype),
    )
    summed_up, summed_down = (
        lax.psum_scatter(
            (local_up + far_up)[None].astype(jnp.bfloat16), "dp", scatter_dimension=1, tiled=True
        ).astype(jnp.float32),
        lax.psum_scatter(
            (local_down + far_down)[None].astype(jnp.bfloat16),
            "dp",
            scatter_dimension=2,
            tiled=True,
        ).astype(jnp.float32),
    )
    return (
        layer_out,
        grad_tokens,
        summed_up.astype(jnp.bfloat16),
        summed_down.astype(jnp.bfloat16),
    )


def solution(mesh):
    return jax.shard_map(
        local,
        mesh=mesh,
        in_specs=(
            P(("dp", "expert"), None),
            P(("dp", "expert"), None),
            P(("dp", "expert"), None),
            P(("dp", "expert"), None),
            P(),
            P("expert", None, None),
            P("expert", None, None),
        ),
        out_specs=(
            P(("dp", "expert"), None),
            P(("dp", "expert"), None),
            P("expert", "dp", None),
            P("expert", None, "dp"),
        ),
        check_vma=False,
    )
```

profile of v0, /device:TPU:1, one launch (start us, length us, event | category | flops | bytes accessed | tf_op | source)
XLA Modules:
  0.0 793.2 jit_solution(6789834141041260389)
XLA Ops:
  12.4 4.3 gather_fusion.2
  16.9 2.8 gather_fusion
  21.3 3.1 broadcast_select_fusion
  24.4 19.5 %all-to-all-start = ((bf16[64,10,1024]{2,1,0:T(8,128)(2,1)}), bf16[64,10,1024]{2,1,0:T(8,128)(2,1)}, u32[]{:S(2)}, u32[]{:S(2)}) async-start(bf16[64,10,1024]{2,1,0:T(8,128)(2,1)} %broadcast_select_fusion), calls=%async_computation | async-start | bytes 4194304 | tf_op jit(solution)/shard_map/all_to_all | solution.py:54
  44.0 2.8 gather_fusion.3
  46.9 2.1 reshape.120
  49.0 3.9 multiply_convert_fusion
  52.9 85.9 %all-to-all-done = bf16[64,10,1024]{2,1,0:T(8,128)(2,1)} async-done(((bf16[64,10,1024]{2,1,0:T(8,128)(2,1)}), bf16[64,10,1024]{2,1,0:T(8,128)(2,1)}, u32[]{:S(2)}, u32[]{:S(2)}) %all-to-all-start) | async-done | bytes 1310752 | tf_op jit(solution)/shard_map/all_to_all | solution.py:54
  138.8 10.8 %all-to-all-start.2 = ((bf16[64,10,1024]{2,1,0:T(8,128)(2,1)}), bf16[64,10,1024]{2,1,0:T(8,128)(2,1)}, u32[]{:S(2)}, u32[]{:S(2)}) async-start(bf16[64,10,1024]{2,1,0:T(8,128)(2,1)} %multiply_convert_fusion), calls=%async_computation.2 | async-start | bytes 4194304 | tf_op jit(solution)/shard_map/all_to_all | solution.py:57
  149.6 2.6 reshape.111
  152.2 2.6 fusion.5
  156.0 2.3 convolution_convert_fusion.1
  158.3 3.6 reshape.112
  161.9 82.1 %all-to-all-done.2 = bf16[64,10,1024]{2,1,0:T(8,128)(2,1)} async-done(((bf16[64,10,1024]{2,1,0:T(8,128)(2,1)}), bf16[64,10,1024]{2,1,0:T(8,128)(2,1)}, u32[]{:S(2)}, u32[]{:S(2)}) %all-to-all-start.2) | async-done | bytes 1310752 | tf_op jit(solution)/shard_map/all_to_all | solution.py:57
  244.0 10.8 %all-to-all-start.1 = ((bf16[64,10,1024]{2,1,0:T(8,128)(2,1)}), bf16[64,10,1024]{2,1,0:T(8,128)(2,1)}, u32[]{:S(2)}, u32[]{:S(2)}) async-start(bf16[64,10,1024]{2,1,0:T(8,128)(2,1)} %reshape.112), calls=%async_computation.1 | async-start | bytes 4194304 | tf_op jit(solution)/shard_map/all_to_all | solution.py:77
  254.9 3.6 reshape.115
  258.6 3.4 fusion.15
  261.9 11.8 %collective-permute-start.1 = (bf16[768,1024]{1,0:T(8,128)(2,1)S(1)}, bf16[768,1024]{1,0:T(8,128)(2,1)S(1)}, u32[]{:S(2)}, u32[]{:S(2)}) collective-permute-start(bf16[768,1024]{1,0:T(8,128)(2,1)S(1)} %get-tuple-element.12), channel_id=1, source_target_pairs={{0,32},{1,33},{2,34},{3,35},{4,36},{5,37},{6,38},{7,39},{8,40},{9,... | collective-permute-start | bytes 4718600 | tf_op jit(solution)/shard_map/ppermute | solution.py:10
  273.8 175.3 %collective-permute-done.1 = bf16[768,1024]{1,0:T(8,128)(2,1)S(1)} collective-permute-done((bf16[768,1024]{1,0:T(8,128)(2,1)S(1)}, bf16[768,1024]{1,0:T(8,128)(2,1)S(1)}, u32[]{:S(2)}, u32[]{:S(2)}) %collective-permute-start.1) | collective-permute-done | bytes 1572896 | tf_op jit(solution)/shard_map/ppermute | solution.py:10
  450.9 8.4 %copy.22 = bf16[1,768,1024]{1,0,2:T(2,128)(2,1)} copy(bf16[1,768,1024]{2,1,0:T(8,128)(2,1)} %fusion.1) | data formatting | bytes 3145728
  459.3 3.4 copy.28
  462.7 3.6 multiply_convert_fusion.1
  467.3 2.3 convolution_convert_fusion
  469.6 3.6 reshape.116
  473.2 46.0 %all-to-all-start.3 = ((bf16[64,10,1024]{2,1,0:T(8,128)(2,1)}), bf16[64,10,1024]{2,1,0:T(8,128)(2,1)}, u32[]{:S(2)}, u32[]{:S(2)}) async-start(bf16[64,10,1024]{2,1,0:T(8,128)(2,1)} %reshape.116), calls=%async_computation.3 | async-start | bytes 4194304 | tf_op jit(solution)/shard_map/all_to_all | solution.py:80
  519.2 2.6 fusion.14
  521.9 11.9 %collective-permute-start = (bf16[1024,768]{1,0:T(8,128)(2,1)S(1)}, bf16[1024,768]{1,0:T(8,128)(2,1)S(1)}, u32[]{:S(2)}, u32[]{:S(2)}) collective-permute-start(bf16[1024,768]{1,0:T(8,128)(2,1)S(1)} %get-tuple-element.10), channel_id=1, source_target_pairs={{0,32},{1,33},{2,34},{3,35},{4,36},{5,37},{6,38},{7,39},{8,40},{9,... | collective-permute-start | bytes 4718600 | tf_op jit(solution)/shard_map/ppermute | solution.py:10
  533.8 180.9 %collective-permute-done = bf16[1024,768]{1,0:T(8,128)(2,1)S(1)} collective-permute-done((bf16[1024,768]{1,0:T(8,128)(2,1)S(1)}, bf16[1024,768]{1,0:T(8,128)(2,1)S(1)}, u32[]{:S(2)}, u32[]{:S(2)}) %collective-permute-start) | collective-permute-done | bytes 1572896 | tf_op jit(solution)/shard_map/ppermute | solution.py:10
  718.4 2.6 reshape.113
  723.8 2.6 reshape.117
  728.6 3.0 reduce_sum.42
  733.7 52.6 %reduce-scatter.5.cloned.1.call-done = bf16[1,128,768]{2,1,0:T(8,128)(2,1)} async-done(((bf16[1,1024,768]{2,1,0:T(8,128)(2,1)}), bf16[1,128,768]{2,1,0:T(8,128)(2,1)}) %reduce-scatter.5.cloned.1.call-update) | async-done | bytes 196624 | tf_op jit(solution)/shard_map/reduce_scatter | solution.py:99
  (52 shorter events, 22.0 us)
Async XLA Ops:
  7.2 148.9 %copy-start = (bf16[1,768,1024]{2,1,0:T(8,128)(2,1)S(1)}, bf16[1,768,1024]{2,1,0:T(8,128)(2,1)}, u32[]{:S(2)}) copy-start(bf16[1,768,1024]{2,1,0:T(8,128)(2,1)} %param.13) | copy-start | bytes 4718596
  12.4 4.5 copy-start.1
  24.4 19.6 %copy-start.2 = (bf16[128,1024]{1,0:T(8,128)(2,1)S(1)}, bf16[128,1024]{1,0:T(8,128)(2,1)}, u32[]{:S(2)}) copy-start(bf16[128,1024]{1,0:T(8,128)(2,1)} %param.8) | copy-start | bytes 786436
  24.4 114.4 %all-to-all-start = ((bf16[64,10,1024]{2,1,0:T(8,128)(2,1)}), bf16[64,10,1024]{2,1,0:T(8,128)(2,1)}, u32[]{:S(2)}, u32[]{:S(2)}) async-start(bf16[64,10,1024]{2,1,0:T(8,128)(2,1)} %broadcast_select_fusion), calls=%async_computation | async-start | bytes 4194304 | tf_op jit(solution)/shard_map/all_to_all | solution.py:54
  138.8 105.3 %all-to-all-start.2 = ((bf16[64,10,1024]{2,1,0:T(8,128)(2,1)}), bf16[64,10,1024]{2,1,0:T(8,128)(2,1)}, u32[]{:S(2)}, u32[]{:S(2)}) async-start(bf16[64,10,1024]{2,1,0:T(8,128)(2,1)} %multiply_convert_fusion), calls=%async_computation.2 | async-start | bytes 4194304 | tf_op jit(solution)/shard_map/all_to_all | solution.py:57
  154.8 1.3 copy-start.6
  244.0 229.1 %all-to-all-start.1 = ((bf16[64,10,1024]{2,1,0:T(8,128)(2,1)}), bf16[64,10,1024]{2,1,0:T(8,128)(2,1)}, u32[]{:S(2)}, u32[]{:S(2)}) async-start(bf16[64,10,1024]{2,1,0:T(8,128)(2,1)} %reshape.112), calls=%async_computation.1 | async-start | bytes 4194304 | tf_op jit(solution)/shard_map/all_to_all | solution.py:77
  254.9 461.4 %reduce-scatter.7.cloned.1.call-start = ((), (), s32[]{:S(2)}) async-start(), calls=%async_computation.7 | async-start | bytes 1769472
  261.9 187.1 %collective-permute-start.1 = (bf16[768,1024]{1,0:T(8,128)(2,1)S(1)}, bf16[768,1024]{1,0:T(8,128)(2,1)S(1)}, u32[]{:S(2)}, u32[]{:S(2)}) collective-permute-start(bf16[768,1024]{1,0:T(8,128)(2,1)S(1)} %get-tuple-element.12), channel_id=1, source_target_pairs={{0,32},{1,33},{2,34},{3,35},{4,36},{5,37},{6,38},{7,39},{8,40},{9,... | collective-permute-start | bytes 4718600 | tf_op jit(solution)/shard_map/ppermute | solution.py:10
  462.7 4.5 copy-start.5
  466.3 1.0 copy-start.4
  473.2 250.7 %all-to-all-start.3 = ((bf16[64,10,1024]{2,1,0:T(8,128)(2,1)}), bf16[64,10,1024]{2,1,0:T(8,128)(2,1)}, u32[]{:S(2)}, u32[]{:S(2)}) async-start(bf16[64,10,1024]{2,1,0:T(8,128)(2,1)} %reshape.116), calls=%async_computation.3 | async-start | bytes 4194304 | tf_op jit(solution)/shard_map/all_to_all | solution.py:80
  519.2 267.1 %reduce-scatter.5.cloned.1.call-start = ((), (), s32[]{:S(2)}) async-start(), calls=%async_computation.6 | async-start | bytes 1769472 | tf_op jit(solution)/shard_map/reduce_scatter | solution.py:99
  521.9 192.8 %collective-permute-start = (bf16[1024,768]{1,0:T(8,128)(2,1)S(1)}, bf16[1024,768]{1,0:T(8,128)(2,1)S(1)}, u32[]{:S(2)}, u32[]{:S(2)}) collective-permute-start(bf16[1024,768]{1,0:T(8,128)(2,1)S(1)} %get-tuple-element.10), channel_id=1, source_target_pairs={{0,32},{1,33},{2,34},{3,35},{4,36},{5,37},{6,38},{7,39},{8,40},{9,... | collective-permute-start | bytes 4718600 | tf_op jit(solution)/shard_map/ppermute | solution.py:10
  727.6 4.1 copy-start.3
Sparse Core Ops, SparseCore 0:
  462.8 71.5 reduce-scatter.6
  716.4 69.9 reduce-scatter.4
where the time goes:
time: 795 us; the launch traced here: 793 us
  waiting for transfers between devices  577 us (73%)
  starting transfers between devices  111 us (14%)
  local copies, waits for them, and re-layouts  57.4 us (7%)
  other arithmetic  16.9 us (2%)
  matrix products  16.8 us (2%)
  between operations  14.4 us (2%)
    ppermute x2, waiting for transfers between devices, shifted(): return lax.ppermute(value, axis, pairs)  356 us
    all_to_all x1, waiting for transfers between devices, local(): lax.all_to_all(send_rows.reshape(block_shape), 'expert', split_axis=0, co...  85.9 us
    all_to_all x1, waiting for transfers between devices, local(): lax.all_to_all(send_cot.reshape(block_shape), 'expert', split_axis=0, con...  82.1 us
    reduce_scatter x1, waiting for transfers between devices, local(): lax.psum_scatter((local_up + far_up)[None].astype(jnp.bfloat16), 'dp', sc...  52.6 us
    all_to_all x1, starting transfers between devices, local(): lax.all_to_all(row_grad.reshape(block_shape), 'expert', split_axis=0, con...  46 us
    ppermute x2, starting transfers between devices, shifted(): return lax.ppermute(value, axis, pairs)  23.7 us
    all_to_all x1, starting transfers between devices, local(): lax.all_to_all(send_rows.reshape(block_shape), 'expert', split_axis=0, co...  19.5 us
    unnamed x20, local copies, waits for them, and re-layouts  17.9 us
  transfers between devices with their start and end apart: 8, of which 5 were waited for; matrix products, arithmetic and copies ran while one was open for 9% of the time, Pallas kernels for 0%

commit v1 on v0

v1 whole, which is shorter than its diff:
```python
import functools

import jax
import jax.numpy as jnp
from jax import lax
from jax.experimental import pallas as pl
from jax.experimental.pallas import tpu as pltpu
from jax.sharding import PartitionSpec as P

MESH = pl.DeviceIdType.MESH
NX = 4
LANES = 128
f32, bf16, i32 = jnp.float32, jnp.bfloat16, jnp.int32


def place():
    dp, ex = lax.axis_index("dp"), lax.axis_index("expert")
    return dp, ex // NX, ex % NX


def z_shift(o, core, w):
    return o - w * ((o + core) // (w // 2 + 1))


def contract(a, b, da, db):
    return lax.dot_general(a, b, (((da,), (db,)), ((), ())), preferred_element_type=f32)


def spread(rows, stage, out_ref, which):
    count, width = rows.shape
    chunks = width // LANES
    for c in range(chunks):
        stage[pl.ds(c, count, stride=chunks), :] = rows[:, c * LANES : (c + 1) * LANES]
    out_ref[which] = stage[...].astype(bf16)


def gather_rows(in_ref, which, stage, chunks):
    stage[...] = in_ref[which].astype(f32)
    count = stage.shape[0] // chunks
    return jnp.concatenate(
        [stage[pl.ds(c, count, stride=chunks), :] for c in range(chunks)], axis=1
    )


def prep_kernel(nz, cap, ids_ref, gates_ref, home_ref, tok_ref, cot_ref, send_ref, sel_ref, stage):
    _, z, x = place()
    w = nz // 2
    tok_count = ids_ref.shape[0]
    experts = home_ref.shape[1]
    rows = experts * cap
    home = home_ref[...]
    shift = NX.bit_length() - 1
    block_z = ((home >> shift) + (nz - z)) & (w - 1)
    block_x = ((home & (NX - 1)) + (NX - x)) & (NX - 1)
    first_row = (block_z * NX + block_x).astype(f32) * float(cap)

    ids = ids_ref[...]
    which = lax.broadcasted_iota(i32, (tok_count, experts), 1)
    earlier = lax.broadcasted_iota(i32, (tok_count, tok_count), 0) > lax.broadcasted_iota(
        i32, (tok_count, tok_count), 1
    )
    earlier = earlier.astype(f32).astype(bf16)
    row_no = lax.broadcasted_iota(i32, (tok_count, rows), 1)
    base = first_row
    sels = []
    for k in range(2):
        hot = (ids[:, k : k + 1] == which).astype(f32)
        before = contract(earlier, hot.astype(bf16), 1, 0)
        row = jnp.sum(hot * (base + before), axis=1, keepdims=True).astype(i32)
        sels.append((row == row_no).astype(f32).astype(bf16))
        base = base + jnp.sum(hot, axis=0, keepdims=True)
    sel_ref[0] = sels[0]
    sel_ref[1] = sels[1]
    spread(contract(sels[0] + sels[1], tok_ref[...], 0, 0), stage, send_ref, 0)
    cot = cot_ref[...].astype(f32)
    scaled = [(gates_ref[:, k : k + 1] * cot).astype(bf16) for k in range(2)]
    picked = contract(sels[0], scaled[0], 0, 0) + contract(sels[1], scaled[1], 0, 0)
    spread(picked, stage, send_ref, 1)


def far_order(i, w):
    k = i // NX
    o = w // 2 + k // 2 - (k % 2) * (2 * (k // 2) + 1)
    return o, NX - 1 - i % NX


def block_refs(src, dst, b, size):
    at = pl.ds(pl.multiple_of(b * size, size), size)
    return src.at[:, at, :], dst.at[:, at, :]


def exchange_blocks(nz, sign, src, dst, send_sem, recv_sem):
    dp, z, x = place()
    core, w = dp % 2, nz // 2
    blocks = w * NX
    size = src.shape[1] // blocks

    def copy(i):
        o, xo = far_order(i, w)
        b = o * NX + xo
        to_z = (z + nz + sign * z_shift(o, core, w)) % nz
        to_x = (x + NX + sign * xo) % NX
        s, d = block_refs(src, dst, b, size)
        return pltpu.make_async_remote_copy(
            src_ref=s,
            dst_ref=d,
            send_sem=send_sem.at[b],
            recv_sem=recv_sem.at[b],
            device_id=(dp, to_z * NX + to_x),
            device_id_type=MESH,
        )

    return copy, blocks - 1


def greet_blocks(nz, sign, barrier):
    dp, z, x = place()
    core, w = dp % 2, nz // 2

    def tell(i, _):
        o, xo = far_order(i, w)
        to_z = (z + nz - sign * z_shift(o, core, w)) % nz
        to_x = (x + NX - sign * xo) % NX
        pl.semaphore_signal(
            barrier, inc=1, device_id=(dp, to_z * NX + to_x), device_id_type=MESH
        )
        return 0

    lax.fori_loop(0, w * NX - 1, tell, 0)
    return w * NX - 1


def each(count, act):
    def step(i, _):
        act(i)
        return 0

    lax.fori_loop(0, count, step, 0)


def dispatch_kernel(nz, send_ref, recv_ref, send_sem, recv_sem, own_sem):
    barrier = pltpu.get_barrier_semaphore()
    size = send_ref.shape[1] // (nz // 2 * NX)
    own = pltpu.make_async_copy(*block_refs(send_ref, recv_ref, 0, size), own_sem)
    own.start()
    pl.semaphore_wait(barrier, greet_blocks(nz, 1, barrier))
    copy, count = exchange_blocks(nz, 1, send_ref, recv_ref, send_sem, recv_sem)
    each(count, lambda i: copy(i).start())
    own.wait()
    each(count, lambda i: copy(i).wait())


def expert_kernel(recv_ref, up_ref, down_ref, ret_ref, gup_ref, gdn_ref, stage):
    up, down = up_ref[...], down_ref[...]
    chunks = up.shape[0] // LANES
    in_f = gather_rows(recv_ref, 0, stage, chunks)
    in_rows = in_f.astype(bf16)
    dy = gather_rows(recv_ref, 1, stage, chunks).astype(bf16)
    pre = contract(in_rows, up, 1, 0)
    sig = 1.0 / (1.0 + jnp.exp(-pre))
    act = (pre * sig).astype(bf16)
    spread(contract(act, down, 1, 0), stage, ret_ref, 0)
    act_grad = contract(dy, down, 1, 1)
    pre_grad = (act_grad * (sig * (1.0 + pre * (1.0 - sig)))).astype(bf16)
    spread(contract(pre_grad, up, 1, 1), stage, ret_ref, 1)
    shards, depth, _ = gup_ref.shape
    for j in range(shards):
        part = in_rows[:, j * depth : (j + 1) * depth]
        gup_ref[j] = contract(part, pre_grad, 0, 0).astype(bf16)
    act_t = act.astype(f32).T.astype(bf16)
    for j in range(0, shards, 2):
        both = contract(act_t, dy[:, j * depth : (j + 2) * depth], 1, 0).astype(bf16)
        gdn_ref[j] = both[:, :depth]
        gdn_ref[j + 1] = both[:, depth:]


def give_back_kernel(
    nz, ret_ref, gup_ref, gdn_ref, back_ref, fup_ref, fdn_ref,
    core_up, core_dn, sum_up, sum_dn, pair_up, pair_dn, mine_up, mine_dn,
    one_up, one_dn, tot_up, tot_dn, far_up, far_dn,
    send_sem, recv_sem, own_sem, s_sem, r_sem,
):
    dp, z, x = place()
    core, y = dp % 2, dp // 2
    ex = z * NX + x
    barrier = pltpu.get_barrier_semaphore()
    size = ret_ref.shape[1] // (nz // 2 * NX)
    partner = (y * 2 + 1 - core, ex)
    flip1, flip3 = y + 1 - 2 * (y % 2), 3 - y
    beside1 = (flip1 * 2 + core, ex)
    beside3 = (flip3 * 2 + core, ex)
    across = (dp, ((z + nz // 2) % nz) * NX + x)

    own = pltpu.make_async_copy(*block_refs(ret_ref, back_ref, 0, size), own_sem)
    own.start()
    for other in (partner, beside1, beside3, across):
        pl.semaphore_signal(barrier, inc=1, device_id=other, device_id_type=MESH)
    pl.semaphore_wait(barrier, 4 + greet_blocks(nz, -1, barrier))

    def remote(n, src, dst, to):
        return pltpu.make_async_remote_copy(
            src_ref=src, dst_ref=dst, send_sem=s_sem.at[n], recv_sem=r_sem.at[n],
            device_id=to, device_id_type=MESH,
        )

    swap_up = remote(0, gup_ref.at[:, 1 - core], core_up, partner)
    swap_dn = remote(1, gdn_ref.at[:, 1 - core], core_dn, partner)
    swap_up.start()
    swap_dn.start()
    copy, count = exchange_blocks(nz, -1, ret_ref, back_ref, send_sem, recv_sem)
    each(count, lambda i: copy(i).start())

    def add(a, b):
        return (a.astype(f32) + b.astype(f32)).astype(bf16)

    first = []
    for n, swap, part, rx, sums, got, near, near_far, far, to in (
        (2, swap_up, gup_ref, core_up, sum_up, pair_up, flip1, 3 - flip1, flip3, beside1),
        (3, swap_dn, gdn_ref, core_dn, sum_dn, pair_dn, flip3, 3 - flip1, flip1, beside3),
    ):
        swap.wait()
        sums[0] = add(part[near, core], rx[near])
        sums[1] = add(part[near_far, core], rx[near_far])
        step = remote(n, sums.at[0:2], got, to)
        step.start()
        sums[2] = add(part[y, core], rx[y])
        sums[3] = add(part[far, core], rx[far])
        first.append(step)
    second = []
    for n, step, sums, got, mine, one, to in (
        (4, first[0], sum_up, pair_up, mine_up, one_up, beside3),
        (5, first[1], sum_dn, pair_dn, mine_dn, one_dn, beside1),
    ):
        step.wait()
        mine[0] = add(sums[3], got[1])
        step = remote(n, mine.at[0], one, to)
        step.start()
        mine[1] = add(sums[2], got[0])
        second.append(step)
    last = []
    for n, step, mine, one, tot, got in (
        (6, second[0], mine_up, one_up, tot_up, far_up),
        (7, second[1], mine_dn, one_dn, tot_dn, far_dn),
    ):
        step.wait()
        tot[...] = add(mine[1], one[...])
        step = remote(n, tot, got, across)
        step.start()
        last.append(step)
    own.wait()
    each(count, lambda i: copy(i).wait())
    for step, tot, got, out in (
        (last[0], tot_up, far_up, fup_ref),
        (last[1], tot_dn, far_dn, fdn_ref),
    ):
        step.wait()
        out[...] = add(tot[...], got[...])


def combine_kernel(back_ref, sel_ref, gates_ref, out_ref, grad_ref, stage):
    chunks = out_ref.shape[1] // LANES
    outs = gather_rows(back_ref, 0, stage, chunks).astype(bf16)
    first, second = sel_ref[0], sel_ref[1]
    total = gates_ref[:, 0:1] * contract(first, outs, 1, 0)
    total = total + gates_ref[:, 1:2] * contract(second, outs, 1, 0)
    out_ref[...] = total.astype(bf16)
    grads = gather_rows(back_ref, 1, stage, chunks).astype(bf16)
    grad_ref[...] = contract(first + second, grads, 1, 0).astype(bf16)


def shape(*dims, dtype=bf16):
    return jax.ShapeDtypeStruct(dims, dtype)


VM = pl.BlockSpec(memory_space=pltpu.VMEM)


def local(nz, ndp, tokens, cotangent, expert_ids, gates, expert_home, up_weight, down_weight):
    tok_count, width = tokens.shape
    hidden = up_weight.shape[2]
    experts = expert_home.shape[0]
    cap = 5 * tok_count * 2 // (4 * experts)
    rows = experts * cap
    chunks = width // LANES
    flat = rows * chunks
    blocks = experts
    depth = width // ndp
    ny = ndp // 2
    stage = pltpu.VMEM((flat, LANES), f32)
    dma = pltpu.SemaphoreType.DMA

    send, sel = pl.pallas_call(
        functools.partial(prep_kernel, nz, cap),
        out_shape=(shape(2, flat, LANES), shape(2, tok_count, rows)),
        in_specs=[VM] * 5,
        out_specs=(VM, VM),
        scratch_shapes=[stage],
        name="prep",
    )(expert_ids, gates, expert_home.reshape(1, experts), tokens, cotangent)

    recv = pl.pallas_call(
        functools.partial(dispatch_kernel, nz),
        out_shape=shape(2, flat, LANES),
        in_specs=[VM],
        out_specs=VM,
        scratch_shapes=[dma((blocks,)), dma((blocks,)), dma],
        compiler_params=pltpu.CompilerParams(collective_id=0, has_side_effects=True),
        name="dispatch",
    )(send)

    ret, gup, gdn = pl.pallas_call(
        expert_kernel,
        out_shape=(shape(2, flat, LANES), shape(ndp, depth, hidden), shape(ndp, hidden, depth)),
        in_specs=[VM] * 3,
        out_specs=(VM,) * 3,
        scratch_shapes=[stage],
        name="experts",
    )(recv, up_weight.reshape(width, hidden), down_weight.reshape(hidden, width))

    def both(*lead):
        return [pltpu.VMEM(lead + (depth, hidden), bf16), pltpu.VMEM(lead + (hidden, depth), bf16)]

    back, fup, fdn = pl.pallas_call(
        functools.partial(give_back_kernel, nz),
        out_shape=(shape(2, flat, LANES), shape(depth, hidden), shape(hidden, depth)),
        in_specs=[VM] * 3,
        out_specs=(VM,) * 3,
        scratch_shapes=both(ny) + both(ny) + both(2) + both(2) + both() + both() + both()
        + [dma((blocks,)), dma((blocks,)), dma, dma((8,)), dma((8,))],
        compiler_params=pltpu.CompilerParams(collective_id=1, has_side_effects=True),
        name="give_back",
    )(ret, gup.reshape(ny, 2, depth, hidden), gdn.reshape(ny, 2, hidden, depth))

    layer_out, grad_tokens = pl.pallas_call(
        combine_kernel,
        out_shape=(shape(tok_count, width), shape(tok_count, width)),
        in_specs=[VM] * 3,
        out_specs=(VM, VM),
        scratch_shapes=[stage],
        name="combine",
    )(back, sel, gates)
    return layer_out, grad_tokens, fup[None], fdn[None]


def solution(mesh):
    rows = P(("dp", "expert"), None)
    held = P("expert", None, None)
    return jax.shard_map(
        functools.partial(local, mesh.shape["expert"] // NX, mesh.shape["dp"]),
        mesh=mesh,
        in_specs=(rows, rows, rows, rows, P(), held, held),
        out_specs=(rows, rows, P("expert", "dp", None), P("expert", None, "dp")),
        check_vma=False,
    )
```

time: 795 us -> 140 us (0.18)
  the two profiles are of different devices: /device:TPU:1 before, /device:TPU:153 now
where the time goes in v1:
time: 140 us
  Pallas kernels  135 us (96%)
  local copies, waits for them, and re-layouts  4.18 us (3%)
    pallas_call x1, Pallas kernels, local(): pl.pallas_call(functools.partial(give_back_kernel, nz), out_shape=(shape(...  77.1 us
    pallas_call x1, Pallas kernels, local(): pl.pallas_call(functools.partial(dispatch_kernel, nz), out_shape=shape(2,...  43.4 us
    pallas_call x1, Pallas kernels, local(): pl.pallas_call(expert_kernel, out_shape=(shape(2, flat, LANES), shape(ndp...  7.88 us
    unnamed x8, local copies, waits for them, and re-layouts  4.18 us
    pallas_call x1, Pallas kernels, local(): pl.pallas_call(functools.partial(prep_kernel, nz, cap), out_shape=(shape(...  3.48 us
    pallas_call x1, Pallas kernels, local(): pl.pallas_call(combine_kernel, out_shape=(shape(tok_count, width), shape(...  3.12 us

profile of v1, /device:TPU:153, one launch (start us, length us, event | category | flops | bytes accessed | tf_op | source)
XLA Modules:
  0.0 139.8 jit_solution(13890481316344991493)
XLA Ops:
  0.6 1.4 %copy.12.gates_ref = f32[128,2]{1,0:T(8,128)} copy(f32[128,2]{0,1:T(2,128)} %param.10) | data formatting | bytes 2048 | tf_op args[3]
  2.0 1.4 %copy.11.ids_ref = s32[128,2]{1,0:T(8,128)} copy(s32[128,2]{0,1:T(2,128)} %param.9) | data formatting | bytes 2048 | tf_op args[2]
  3.4 3.5 %prep.1 = (bf16[2,2560,128]{2,1,0:T(8,128)(2,1)}, bf16[2,128,320]{2,1,0:T(8,128)(2,1)}) custom-call(s32[128,2]{1,0:T(8,128)} %copy.11.ids_ref, f32[128,2]{1,0:T(8,128)} %copy.12.gates_ref, s32[1,32]{1,0:T(1,128)} %bitcast.13, bf16[128,1024]{1,0:T(8,128)(2,1)} %tok_ref.1, bf16[128,1024]{1,0:T(8,128)(2,1)} %cot_ref.1), custom_call_target="tpu_custom_call" | custom-call | tf_op jit(solution)/shard_map/prep/pallas_call | solution.py:292
  6.9 43.4 %dispatch.1.recv_ref = bf16[2,2560,128]{2,1,0:T(8,128)(2,1)} custom-call(bf16[2,2560,128]{2,1,0:T(8,128)(2,1)} %get-tuple-element.14.send_ref), custom_call_target="tpu_custom_call" | custom-call | tf_op jit(solution)/shard_map/dispatch/pallas_call | solution.py:301
  50.3 7.9 %experts.1 = (bf16[2,2560,128]{2,1,0:T(8,128)(2,1)}, bf16[8,128,768]{2,1,0:T(8,128)(2,1)}, bf16[8,768,128]{2,1,0:T(8,128)(2,1)}) custom-call(bf16[2,2560,128]{2,1,0:T(8,128)(2,1)} %dispatch.1.recv_ref, bf16[1024,768]{1,0:T(8,128)(2,1)} %bitcast.7, bf16[768,1024]{1,0:T(8,128)(2,1)} %bitcast.8), custom_call_target="tpu_custom_call" | custom-call | tf_op jit(solution)/shard_map/experts/pallas_call | solution.py:311
  58.2 77.1 %give_back.1 = (bf16[2,2560,128]{2,1,0:T(8,128)(2,1)}, bf16[128,768]{1,0:T(8,128)(2,1)}, bf16[768,128]{1,0:T(8,128)(2,1)}) custom-call(bf16[2,2560,128]{2,1,0:T(8,128)(2,1)} %get-tuple-element.15.ret_ref, bf16[4,2,128,768]{3,2,1,0:T(8,128)(2,1)} %bitcast.9, bf16[4,2,768,128]{3,2,1,0:T(8,128)(2,1)} %bitcast.10), custom_call_target="tpu_custom_call" | custom-call | tf_op jit(solution)/shard_map/give_back/pallas_call | solution.py:323
  135.3 0.0 copy-start.1
  135.3 0.0 copy-start
  135.3 3.1 %combine.1 = (bf16[128,1024]{1,0:T(8,128)(2,1)}, bf16[128,1024]{1,0:T(8,128)(2,1)}) custom-call(bf16[2,2560,128]{2,1,0:T(8,128)(2,1)} %get-tuple-element.18.back_ref, bf16[2,128,320]{2,1,0:T(8,128)(2,1)} %get-tuple-element.19.sel_ref, f32[128,2]{1,0:T(8,128)} %copy.12.gates_ref), custom_call_target="tpu_custom_call" | custom-call | tf_op jit(solution)/shard_map/combine/pallas_call | solution.py:334
  138.4 0.0 copy-done.1
  138.4 0.7 copy.16
  139.1 0.0 copy-done
  139.1 0.7 copy.17
Async XLA Ops:
  135.3 3.1 %copy-start.1 = (bf16[128,768]{1,0:T(8,128)(2,1)S(1)}, bf16[128,768]{1,0:T(8,128)(2,1)}, u32[]{:S(2)}) copy-start(bf16[128,768]{1,0:T(8,128)(2,1)} %get-tuple-element.22) | copy-start | bytes 589828
  135.3 3.8 %copy-start = (bf16[768,128]{1,0:T(8,128)(2,1)S(1)}, bf16[768,128]{1,0:T(8,128)(2,1)}, u32[]{:S(2)}) copy-start(bf16[768,128]{1,0:T(8,128)(2,1)} %get-tuple-element.23) | copy-start | bytes 589828

commit v2 on v1

v2 whole, which is shorter than its diff:
```python
import functools

import jax
import jax.numpy as jnp
from jax import lax
from jax.experimental import pallas as pl
from jax.experimental.pallas import tpu as pltpu
from jax.sharding import PartitionSpec as P

MESH = pl.DeviceIdType.MESH
NX = 4
LANES = 128
f32, bf16, i32 = jnp.float32, jnp.bfloat16, jnp.int32


def place():
    dp, ex = lax.axis_index("dp"), lax.axis_index("expert")
    return dp, ex // NX, ex % NX


def z_shift(o, core, w):
    return o - w * ((o + core) // (w // 2 + 1))


def contract(a, b, da, db):
    return lax.dot_general(a, b, (((da,), (db,)), ((), ())), preferred_element_type=f32)


def spread(rows, stage, out_ref):
    count, width = rows.shape
    chunks = width // LANES
    for c in range(chunks):
        stage[pl.ds(c, count, stride=chunks), :] = rows[:, c * LANES : (c + 1) * LANES]
    out_ref[...] = stage[...].astype(bf16)


def gather_rows(flat, stage, chunks):
    stage[...] = flat.astype(f32)
    count = stage.shape[0] // chunks
    parts = [stage[pl.ds(c, count, stride=chunks), :] for c in range(chunks)]
    return jnp.concatenate(parts, axis=1).astype(bf16)


def iota(shape, dim):
    return lax.broadcasted_iota(i32, shape, dim)


def as_column(row):
    n = row.shape[1]
    eye = iota((n, n), 0) == iota((n, n), 1)
    return jnp.sum(jnp.where(eye, row, 0.0), axis=1, keepdims=True)


def selections(nz, cap, ids, home):
    _, z, x = place()
    w = nz // 2
    tok_count, experts = ids.shape[1], home.shape[1]
    rows = experts * cap
    slot = as_column(home.astype(f32)).astype(i32)
    shift = NX.bit_length() - 1
    block_z = ((slot >> shift) + (nz - z)) & (w - 1)
    block_x = ((slot & (NX - 1)) + (NX - x)) & (NX - 1)
    base = (block_z * NX + block_x).astype(f32) * float(cap)
    earlier = iota((tok_count, tok_count), 0) < iota((tok_count, tok_count), 1)
    earlier = earlier.astype(f32).astype(bf16)
    row_no = iota((rows, tok_count), 0)
    sels = []
    for k in range(2):
        hot = (iota((experts, tok_count), 0) == ids[k : k + 1, :]).astype(f32)
        before = contract(hot.astype(bf16), earlier, 1, 0)
        row = jnp.sum(hot * (base + before), axis=0, keepdims=True).astype(i32)
        sels.append((row_no == row).astype(f32).astype(bf16))
        base = base + jnp.sum(hot, axis=1, keepdims=True)
    return sels


def far_order(i, w):
    k = i // NX
    o = w // 2 + k // 2 - (k % 2) * (2 * (k // 2) + 1)
    return o, NX - 1 - i % NX


def peer(nz, sign, i):
    dp, z, x = place()
    w = nz // 2
    o, xo = far_order(i, w)
    to_z = (z + nz + sign * z_shift(o, dp % 2, w)) % nz
    to_x = (x + NX + sign * xo) % NX
    return o * NX + xo, (dp, to_z * NX + to_x)


def each(count, act):
    def step(i, _):
        act(i)
        return 0

    lax.fori_loop(0, count, step, 0)


def add(a, b):
    return (a.astype(f32) + b.astype(f32)).astype(bf16)


def layer_kernel(
    nz, cap, subs,
    ids_ref, gates_ref, home_ref, tok_hbm, cot_hbm, up_hbm, down_hbm,
    back_ref, sel_ref, tot_up, tot_dn, far_up, far_dn,
    tok_ref, cot_ref, up_ref, down_ref, stage, send_x, send_y, recv_x, recv_y, ret_x, ret_y,
    part_up, part_dn, core_up, core_dn, sum_up, sum_dn, pair_up, pair_dn,
    mine_up, mine_dn, one_up, one_dn, ring_up, ring_dn,
    in_sem, block_send, block_recv, s_sem, r_sem, ring_send, ring_recv,
):
    dp, z, x = place()
    core, y = dp % 2, dp // 2
    ex = z * NX + x
    blocks = nz // 2 * NX
    others = blocks - 1
    size = send_x.shape[0] // blocks
    partner = (y * 2 + 1 - core, ex)
    flip1, flip3 = y + 1 - 2 * (y % 2), 3 - y
    beside1 = (flip1 * 2 + core, ex)
    beside3 = (flip3 * 2 + core, ex)

    barrier = pltpu.get_barrier_semaphore()

    def tell(to):
        pl.semaphore_signal(barrier, inc=1, device_id=to, device_id_type=MESH)

    def tell_both(i):
        tell(peer(nz, 1, i)[1])
        tell(peer(nz, -1, i)[1])

    each(others, tell_both)
    for to in (partner, beside1, beside3):
        tell(to)
    loads = [
        pltpu.make_async_copy(src, dst, in_sem.at[n])
        for n, (src, dst) in enumerate(
            ((tok_hbm, tok_ref), (cot_hbm, cot_ref), (up_hbm, up_ref), (down_hbm, down_ref))
        )
    ]
    for load in loads:
        load.start()

    def block_copy(n, sign, src, dst):
        def copy(i):
            b, to = peer(nz, sign, i)
            at = pl.ds(pl.multiple_of(b * size, size), size)
            return pltpu.make_async_remote_copy(
                src_ref=src.at[at, :], dst_ref=dst.at[at, :],
                send_sem=block_send.at[n, b], recv_sem=block_recv.at[n, b],
                device_id=to, device_id_type=MESH,
            )

        return copy

    give_x = block_copy(0, 1, send_x, recv_x)
    give_y = block_copy(1, 1, send_y, recv_y)
    return_x = block_copy(2, -1, ret_x, back_ref.at[0])
    return_y = block_copy(3, -1, ret_y, back_ref.at[1])

    def remote(n, src, dst, to):
        return pltpu.make_async_remote_copy(
            src_ref=src, dst_ref=dst, send_sem=s_sem.at[n], recv_sem=r_sem.at[n],
            device_id=to, device_id_type=MESH,
        )

    first, second = selections(nz, cap, ids_ref[...], home_ref[...])
    sel_ref[0] = first
    sel_ref[1] = second
    loads[0].wait()
    spread(contract(first + second, tok_ref[...], 1, 0), stage, send_x)
    pl.semaphore_wait(barrier, 2 * others + 3)
    each(others, lambda i: give_x(i).start())
    recv_x[0:size, :] = send_x[0:size, :]
    loads[1].wait()
    cot = cot_ref[...].astype(f32)
    picked = contract(first, (as_column(gates_ref[0:1, :]) * cot).astype(bf16), 1, 0)
    picked += contract(second, (as_column(gates_ref[1:2, :]) * cot).astype(bf16), 1, 0)
    spread(picked, stage, send_y)
    each(others, lambda i: give_y(i).start())
    recv_y[0:size, :] = send_y[0:size, :]

    loads[2].wait()
    loads[3].wait()
    chunks = up_ref.shape[0] // LANES
    each(others, lambda i: give_x(i).wait_recv())
    in_rows = gather_rows(recv_x[...], stage, chunks)
    pre = contract(in_rows, up_ref[...], 1, 0)
    sig = 1.0 / (1.0 + jnp.exp(-pre))
    act_wide = pre * sig
    slope = sig * (1.0 + pre * (1.0 - sig))
    spread(contract(act_wide.astype(bf16), down_ref[...], 1, 0), stage, ret_x)
    act_t = act_wide.T.astype(bf16)
    back_ref[0, 0:size, :] = ret_x[0:size, :]

    each(others, lambda i: give_y(i).wait_recv())
    each(others, lambda i: return_x(i).start())
    dy = gather_rows(recv_y[...], stage, chunks)
    pre_grad = (contract(dy, down_ref[...], 1, 1) * slope).astype(bf16)
    ny, _, depth, _ = part_up.shape
    for j in range(2 * ny):
        cut = in_rows[:, j * depth : (j + 1) * depth]
        part_up[j // 2, j % 2] = contract(cut, pre_grad, 0, 0).astype(bf16)
    swap_up = remote(0, part_up.at[:, 1 - core], core_up, partner)
    swap_up.start()
    for j in range(ny):
        two = contract(act_t, dy[:, 2 * j * depth : (2 * j + 2) * depth], 1, 0).astype(bf16)
        part_dn[j, 0] = two[:, :depth]
        part_dn[j, 1] = two[:, depth:]
    swap_dn = remote(1, part_dn.at[:, 1 - core], core_dn, partner)
    swap_dn.start()
    spread(contract(pre_grad, up_ref[...], 1, 1), stage, ret_y)
    each(others, lambda i: return_y(i).start())
    back_ref[1, 0:size, :] = ret_y[0:size, :]

    steps = []
    for n, swap, part, rx, sums, got, near, near_far, far, to in (
        (2, swap_up, part_up, core_up, sum_up, pair_up, flip1, 3 - flip1, flip3, beside1),
        (3, swap_dn, part_dn, core_dn, sum_dn, pair_dn, flip3, 3 - flip1, flip1, beside3),
    ):
        swap.wait()
        sums[0] = add(part[near, core], rx[near])
        sums[1] = add(part[near_far, core], rx[near_far])
        step = remote(n, sums.at[0:2], got, to)
        step.start()
        sums[2] = add(part[y, core], rx[y])
        sums[3] = add(part[far, core], rx[far])
        steps.append(step)
    later = []
    for n, step, sums, got, mine, one, to in (
        (4, steps[0], sum_up, pair_up, mine_up, one_up, beside3),
        (5, steps[1], sum_dn, pair_dn, mine_dn, one_dn, beside1),
    ):
        step.wait()
        mine[0] = add(sums[3], got[1])
        step = remote(n, mine.at[0], one, to)
        step.start()
        mine[1] = add(sums[2], got[0])
        later.append(step)

    half = nz // 2

    def hop(d, j, src, k):
        total, ring = ((tot_up, ring_up), (tot_dn, ring_dn))[d]
        rows = total.shape[0] // subs
        at = pl.ds(j * rows, rows)
        to_z = (z + (1, nz - 1)[d]) % nz
        return pltpu.make_async_remote_copy(
            src_ref=total.at[at] if src is None else ring.at[src, at],
            dst_ref=ring.at[k, at],
            send_sem=ring_send.at[d, k, j], recv_sem=ring_recv.at[d, k, j],
            device_id=(dp, to_z * NX + x), device_id_type=MESH,
        )

    for d, (step, mine, one, tot) in enumerate(
        ((later[0], mine_up, one_up, tot_up), (later[1], mine_dn, one_dn, tot_dn))
    ):
        step.wait()
        tot[...] = add(mine[1], one[...])
        for j in range(subs):
            hop(d, j, None, 0).start()
    both = [(d, j) for j in range(subs) for d in range(2)]

    def forward(k):
        for d, j in both:
            hop(d, j, k, k).wait_recv()
            hop(d, j, k, k + 1).start()

    each(half - 1, forward)
    for d, j in both:
        hop(d, j, half - 1, half - 1).wait_recv()
    far_up[...] = ring_up[half - 1]
    far_dn[...] = ring_dn[half - 1]

    def drain(k):
        for d, j in both:
            hop(d, j, k, k).wait_send()

    each(half, drain)
    for give in (give_x, give_y):
        each(others, lambda i: give(i).wait_send())
    for give in (return_x, return_y):
        each(others, lambda i: give(i).wait())


def combine_kernel(
    back_ref, sel_ref, gates_ref, tot_up, tot_dn, far_up, far_dn,
    out_ref, grad_ref, fup_ref, fdn_ref, stage,
):
    chunks = out_ref.shape[1] // LANES
    outs = gather_rows(back_ref[0], stage, chunks)
    first, second = sel_ref[0], sel_ref[1]
    total = as_column(gates_ref[0:1, :]) * contract(first, outs, 0, 0)
    total += as_column(gates_ref[1:2, :]) * contract(second, outs, 0, 0)
    out_ref[...] = total.astype(bf16)
    grads = gather_rows(back_ref[1], stage, chunks)
    grad_ref[...] = contract(first + second, grads, 0, 0).astype(bf16)
    fup_ref[...] = add(tot_up[...], far_up[...])
    fdn_ref[...] = add(tot_dn[...], far_dn[...])


def shape(*dims, dtype=bf16):
    return jax.ShapeDtypeStruct(dims, dtype)


VM = pl.BlockSpec(memory_space=pltpu.VMEM)
HBM = pl.BlockSpec(memory_space=pl.ANY)
SUBS = 4


def local(nz, ndp, tokens, cotangent, expert_ids, gates, expert_home, up_weight, down_weight):
    tok_count, width = tokens.shape
    hidden = up_weight.shape[2]
    experts = expert_home.shape[0]
    cap = 5 * tok_count * 2 // (4 * experts)
    rows = experts * cap
    flat = rows * (width // LANES)
    depth = width // ndp
    ny = ndp // 2
    half = nz // 2
    stage = pltpu.VMEM((flat, LANES), f32)
    dma = pltpu.SemaphoreType.DMA
    up_shape, dn_shape = (depth, hidden), (hidden, depth)

    def both(*lead):
        return [pltpu.VMEM(lead + up_shape, bf16), pltpu.VMEM(lead + dn_shape, bf16)]

    gates_t = gates.T
    back, sel, *totals = pl.pallas_call(
        functools.partial(layer_kernel, nz, cap, SUBS),
        out_shape=(shape(2, flat, LANES), shape(2, rows, tok_count))
        + (shape(*up_shape), shape(*dn_shape)) * 2,
        in_specs=[VM] * 3 + [HBM] * 4,
        out_specs=(VM,) * 6,
        scratch_shapes=[
            pltpu.VMEM((tok_count, width), bf16),
            pltpu.VMEM((tok_count, width), bf16),
            pltpu.VMEM((width, hidden), bf16),
            pltpu.VMEM((hidden, width), bf16),
            stage,
        ]
        + [pltpu.VMEM((flat, LANES), bf16)] * 6
        + both(ny, 2) + both(ny) + both(ny) + both(2) + both(2) + both() + both(half)
        + [
            dma((4,)), dma((4, experts)), dma((4, experts)), dma((6,)), dma((6,)),
            dma((2, half, SUBS)), dma((2, half, SUBS)),
        ],
        compiler_params=pltpu.CompilerParams(collective_id=0, has_side_effects=True),
        name="layer",
    )(
        expert_ids.T, gates_t, expert_home.reshape(1, experts), tokens, cotangent,
        up_weight.reshape(width, hidden), down_weight.reshape(hidden, width),
    )

    layer_out, grad_tokens, fup, fdn = pl.pallas_call(
        combine_kernel,
        out_shape=(shape(tok_count, width),) * 2 + (shape(*up_shape), shape(*dn_shape)),
        in_specs=[VM] * 7,
        out_specs=(VM,) * 4,
        scratch_shapes=[stage],
        name="combine",
    )(back, sel, gates_t, *totals)
    return layer_out, grad_tokens, fup[None], fdn[None]


def solution(mesh):
    rows = P(("dp", "expert"), None)
    held = P("expert", None, None)
    return jax.shard_map(
        functools.partial(local, mesh.shape["expert"] // NX, mesh.shape["dp"]),
        mesh=mesh,
        in_specs=(rows, rows, rows, rows, P(), held, held),
        out_specs=(rows, rows, P("expert", "dp", None), P("expert", None, "dp")),
        check_vma=False,
    )
```

time: 140 us -> 123 us (0.88)
  the two profiles are of different devices: /device:TPU:153 before, /device:TPU:1 now
where the time goes in v2:
time: 123 us
  Pallas kernels  122 us (99%)
    pallas_call x1, Pallas kernels, local(): pl.pallas_call(functools.partial(layer_kernel, nz, cap, SUBS), out_shape=...  119 us
    pallas_call x1, Pallas kernels, local(): pl.pallas_call(combine_kernel, out_shape=(shape(tok_count, width),) * 2 +...  3.44 us

profile of v2, /device:TPU:1, one launch (start us, length us, event | category | flops | bytes accessed | tf_op | source)
XLA Modules:
  0.0 122.8 jit_solution(8640251511423507361)
XLA Ops:
  0.6 118.7 %layer.1 = (bf16[2,2560,128]{2,1,0:T(8,128)(2,1)}, bf16[2,320,128]{2,1,0:T(8,128)(2,1)}, bf16[128,768]{1,0:T(8,128)(2,1)}, bf16[768,128]{1,0:T(8,128)(2,1)}, bf1...) custom-call(s32[2,128]{1,0:T(2,128)} %bitcast.11, f32[2,128]{1,0:T(2,128)} %bitcast.9, s32[1,32]{1,0:T(1,128)} %bitcast.12, ...), custom_call_target="tpu_custom_call" | custom-call | tf_op jit(solution)/shard_map/layer/pallas_call | solution.py:330
  119.4 3.4 %combine.1 = (bf16[128,1024]{1,0:T(8,128)(2,1)}, bf16[128,1024]{1,0:T(8,128)(2,1)}, bf16[128,768]{1,0:T(8,128)(2,1)}, bf16[768,128]{1,0:T(8,128)(2,1)}) custom-call(bf16[2,2560,128]{2,1,0:T(8,128)(2,1)} %get-tuple-element.14.back_ref, bf16[2,320,128]{2,1,0:T(8,128)(2,1)} %get-tuple-element.15.sel_ref, f32[2,128]{1,0:T(2,128)} %bitcast.10, ...), custom_call_target="tpu_custom_call" | custom-call | tf_op jit(solution)/shard_map/combine/pallas_call | solution.py:356

commit v3 on v2

--- a/solution.py
+++ b/solution.py
@@ -89,12 +89,12 @@
     return o * NX + xo, (dp, to_z * NX + to_x)
 
 
-def each(count, act):
+def each(count, act, start=0):
     def step(i, _):
         act(i)
         return 0
 
-    lax.fori_loop(0, count, step, 0)
+    lax.fori_loop(start, count, step, 0)
 
 
 def add(a, b):
@@ -102,10 +102,11 @@
 
 
 def layer_kernel(
-    nz, cap, subs,
+    nz, cap, subs, early,
     ids_ref, gates_ref, home_ref, tok_hbm, cot_hbm, up_hbm, down_hbm,
-    back_ref, sel_ref, tot_up, tot_dn, far_up, far_dn,
+    out_ref, grad_ref, fup_ref, fdn_ref,
     tok_ref, cot_ref, up_ref, down_ref, stage, send_x, send_y, recv_x, recv_y, ret_x, ret_y,
+    back_x, back_y, tot_up, tot_dn,
     part_up, part_dn, core_up, core_dn, sum_up, sum_dn, pair_up, pair_dn,
     mine_up, mine_dn, one_up, one_dn, ring_up, ring_dn,
     in_sem, block_send, block_recv, s_sem, r_sem, ring_send, ring_recv,
@@ -156,8 +157,8 @@
 
     give_x = block_copy(0, 1, send_x, recv_x)
     give_y = block_copy(1, 1, send_y, recv_y)
-    return_x = block_copy(2, -1, ret_x, back_ref.at[0])
-    return_y = block_copy(3, -1, ret_y, back_ref.at[1])
+    return_x = block_copy(2, -1, ret_x, back_x)
+    return_y = block_copy(3, -1, ret_y, back_y)
 
     def remote(n, src, dst, to):
         return pltpu.make_async_remote_copy(
@@ -166,8 +167,6 @@
         )
 
     first, second = selections(nz, cap, ids_ref[...], home_ref[...])
-    sel_ref[0] = first
-    sel_ref[1] = second
     loads[0].wait()
     spread(contract(first + second, tok_ref[...], 1, 0), stage, send_x)
     pl.semaphore_wait(barrier, 2 * others + 3)
@@ -192,10 +191,11 @@
     slope = sig * (1.0 + pre * (1.0 - sig))
     spread(contract(act_wide.astype(bf16), down_ref[...], 1, 0), stage, ret_x)
     act_t = act_wide.T.astype(bf16)
-    back_ref[0, 0:size, :] = ret_x[0:size, :]
+    back_x[0:size, :] = ret_x[0:size, :]
+    each(early, lambda i: return_x(i).start())
 
     each(others, lambda i: give_y(i).wait_recv())
-    each(others, lambda i: return_x(i).start())
+    each(others, lambda i: return_x(i).start(), early)
     dy = gather_rows(recv_y[...], stage, chunks)
     pre_grad = (contract(dy, down_ref[...], 1, 1) * slope).astype(bf16)
     ny, _, depth, _ = part_up.shape
@@ -212,7 +212,7 @@
     swap_dn.start()
     spread(contract(pre_grad, up_ref[...], 1, 1), stage, ret_y)
     each(others, lambda i: return_y(i).start())
-    back_ref[1, 0:size, :] = ret_y[0:size, :]
+    back_y[0:size, :] = ret_y[0:size, :]
 
     steps = []
     for n, swap, part, rx, sums, got, near, near_far, far, to in (
@@ -220,24 +220,30 @@
         (3, swap_dn, part_dn, core_dn, sum_dn, pair_dn, flip3, 3 - flip1, flip1, beside3),
     ):
         swap.wait()
+        sums[1] = add(part[near_far, core], rx[near_far])
+        pair = [remote(n, sums.at[1], got.at[1], to), remote(n + 4, sums.at[0], got.at[0], to)]
+        pair[0].start()
         sums[0] = add(part[near, core], rx[near])
-        sums[1] = add(part[near_far, core], rx[near_far])
-        step = remote(n, sums.at[0:2], got, to)
-        step.start()
+        pair[1].start()
+        sums[3] = add(part[far, core], rx[far])
         sums[2] = add(part[y, core], rx[y])
-        sums[3] = add(part[far, core], rx[far])
-        steps.append(step)
+        steps.append(pair)
     later = []
-    for n, step, sums, got, mine, one, to in (
+    for n, pair, sums, got, mine, one, to in (
         (4, steps[0], sum_up, pair_up, mine_up, one_up, beside3),
         (5, steps[1], sum_dn, pair_dn, mine_dn, one_dn, beside1),
     ):
-        step.wait()
+        pair[0].wait()
         mine[0] = add(sums[3], got[1])
         step = remote(n, mine.at[0], one, to)
         step.start()
+        later.append(step)
+    for pair, sums, got, mine in (
+        (steps[0], sum_up, pair_up, mine_up),
+        (steps[1], sum_dn, pair_dn, mine_dn),
+    ):
+        pair[1].wait()
         mine[1] = add(sums[2], got[0])
-        later.append(step)
 
     half = nz // 2
 
@@ -268,36 +274,38 @@
             hop(d, j, k, k + 1).start()
 
     each(half - 1, forward)
+    each(others, lambda i: return_x(i).wait_recv())
+    outs = gather_rows(back_x[...], stage, chunks)
+    total = as_column(gates_ref[0:1, :]) * contract(first, outs, 0, 0)
+    total += as_column(gates_ref[1:2, :]) * contract(second, outs, 0, 0)
+    out_ref[...] = total.astype(bf16)
+    each(others, lambda i: return_y(i).wait_recv())
+    grads = gather_rows(back_y[...], stage, chunks)
+    grad_ref[...] = contract(first + second, grads, 0, 0).astype(bf16)
     for d, j in both:
         hop(d, j, half - 1, half - 1).wait_recv()
-    far_up[...] = ring_up[half - 1]
-    far_dn[...] = ring_dn[half - 1]
+    fup_ref[...] = add(tot_up[...], ring_up[half - 1])
+    fdn_ref[...] = add(tot_dn[...], ring_dn[half - 1])
 
     def drain(k):
         for d, j in both:
             hop(d, j, k, k).wait_send()
 
     each(half, drain)
-    for give in (give_x, give_y):
-        each(others, lambda i: give(i).wait_send())
-    for give in (return_x, return_y):
-        each(others, lambda i: give(i).wait())
-
-
-def combine_kernel(
-    back_ref, sel_ref, gates_ref, tot_up, tot_dn, far_up, far_dn,
-    out_ref, grad_ref, fup_ref, fdn_ref, stage,
-):
-    chunks = out_ref.shape[1] // LANES
-    outs = gather_rows(back_ref[0], stage, chunks)
-    first, second = sel_ref[0], sel_ref[1]
-    total = as_column(gates_ref[0:1, :]) * contract(first, outs, 0, 0)
-    total += as_column(gates_ref[1:2, :]) * contract(second, outs, 0, 0)
-    out_ref[...] = total.astype(bf16)
-    grads = gather_rows(back_ref[1], stage, chunks)
-    grad_ref[...] = contract(first + second, grads, 0, 0).astype(bf16)
-    fup_ref[...] = add(tot_up[...], far_up[...])
-    fdn_ref[...] = add(tot_dn[...], far_dn[...])
+    for moved in (give_x, give_y, return_x, return_y):
+        each(others, lambda i: moved(i).wait_send())
+
+
+def hand_on_kernel(*refs):
+    *arrays, sem = refs
+    half = len(arrays) // 2
+    copies = [
+        pltpu.make_async_copy(arrays[n], arrays[half + n], sem.at[n]) for n in range(half)
+    ]
+    for copy in copies:
+        copy.start()
+    for copy in copies:
+        copy.wait()
 
 
 def shape(*dims, dtype=bf16):
@@ -305,8 +313,10 @@
 
 
 VM = pl.BlockSpec(memory_space=pltpu.VMEM)
-HBM = pl.BlockSpec(memory_space=pl.ANY)
+HBM = pl.BlockSpec(memory_space=pltpu.HBM)
 SUBS = 4
+LAYER_VMEM, HAND_VMEM = 54150 * 1024, 2**20
+EARLY = 10
 
 
 def local(nz, ndp, tokens, cotangent, expert_ids, gates, expert_home, up_weight, down_weight):
@@ -326,13 +336,13 @@
     def both(*lead):
         return [pltpu.VMEM(lead + up_shape, bf16), pltpu.VMEM(lead + dn_shape, bf16)]
 
-    gates_t = gates.T
-    back, sel, *totals = pl.pallas_call(
-        functools.partial(layer_kernel, nz, cap, SUBS),
-        out_shape=(shape(2, flat, LANES), shape(2, rows, tok_count))
-        + (shape(*up_shape), shape(*dn_shape)) * 2,
+    results = (shape(tok_count, width),) * 2 + (shape(*up_shape), shape(*dn_shape))
+    early = min(EARLY, experts - 1)
+    made = pl.pallas_call(
+        functools.partial(layer_kernel, nz, cap, SUBS, early),
+        out_shape=results,
         in_specs=[VM] * 3 + [HBM] * 4,
-        out_specs=(VM,) * 6,
+        out_specs=(VM,) * 4,
         scratch_shapes=[
             pltpu.VMEM((tok_count, width), bf16),
             pltpu.VMEM((tok_count, width), bf16),
@@ -340,27 +350,29 @@
             pltpu.VMEM((hidden, width), bf16),
             stage,
         ]
-        + [pltpu.VMEM((flat, LANES), bf16)] * 6
-        + both(ny, 2) + both(ny) + both(ny) + both(2) + both(2) + both() + both(half)
+        + [pltpu.VMEM((flat, LANES), bf16)] * 8
+        + both() + both(ny, 2) + both(ny) + both(ny) + both(2) + both(2) + both() + both(half)
         + [
-            dma((4,)), dma((4, experts)), dma((4, experts)), dma((6,)), dma((6,)),
+            dma((4,)), dma((4, experts)), dma((4, experts)), dma((8,)), dma((8,)),
             dma((2, half, SUBS)), dma((2, half, SUBS)),
         ],
-        compiler_params=pltpu.CompilerParams(collective_id=0, has_side_effects=True),
+        compiler_params=pltpu.CompilerParams(
+            collective_id=0, has_side_effects=True, vmem_limit_bytes=LAYER_VMEM
+        ),
         name="layer",
     )(
-        expert_ids.T, gates_t, expert_home.reshape(1, experts), tokens, cotangent,
+        expert_ids.T, gates.T, expert_home.reshape(1, experts), tokens, cotangent,
         up_weight.reshape(width, hidden), down_weight.reshape(hidden, width),
     )
-
     layer_out, grad_tokens, fup, fdn = pl.pallas_call(
-        combine_kernel,
-        out_shape=(shape(tok_count, width),) * 2 + (shape(*up_shape), shape(*dn_shape)),
-        in_specs=[VM] * 7,
-        out_specs=(VM,) * 4,
-        scratch_shapes=[stage],
-        name="combine",
-    )(back, sel, gates_t, *totals)
+        hand_on_kernel,
+        out_shape=results,
+        in_specs=[VM] * 4,
+        out_specs=(HBM,) * 4,
+        scratch_shapes=[dma((4,))],
+        compiler_params=pltpu.CompilerParams(vmem_limit_bytes=HAND_VMEM),
+        name="hand_on",
+    )(*made)
     return layer_out, grad_tokens, fup[None], fdn[None]
 
 

time: 123 us -> 119 us (0.967)
  Pallas kernels: 122 us -> 116 us
  local copies, waits for them, and re-layouts: 0 us -> 2.01 us
    pallas_call x2, Pallas kernels: 122 us -> 116 us  [the longest x1 115 us: local(): pl.pallas_call(functools.partial(layer_kernel, nz, cap, SUBS, early), out...]
    unnamed x0 -> x6, local copies, waits for them, and re-layouts: none -> 2.01 us
where the time goes in v3:
time: 119 us
  Pallas kernels  116 us (97%)
  local copies, waits for them, and re-layouts  2.01 us (2%)
    pallas_call x1, Pallas kernels, local(): pl.pallas_call(functools.partial(layer_kernel, nz, cap, SUBS, early), out...  115 us

profile of v3, /device:TPU:1, one launch (start us, length us, event | category | flops | bytes accessed | tf_op | source)
XLA Modules:
  0.0 118.7 jit_solution(13019685718000262065)
XLA Ops:
  0.6 0.0 copy-start
  0.6 0.7 copy-done
  1.3 0.0 copy-start.1
  1.3 0.7 copy-done.1
  2.0 0.0 copy-start.2
  2.0 0.7 copy-done.2
  2.6 115.1 %layer.1 = (bf16[128,1024]{1,0:T(8,128)(2,1)S(1)}, bf16[128,1024]{1,0:T(8,128)(2,1)S(1)}, bf16[128,768]{1,0:T(8,128)(2,1)S(1)}, bf16[768,128]{1,0:T(8,128)(2,1)S(1)}) custom-call(s32[2,128]{1,0:T(2,128)S(1)} %bitcast.7, f32[2,128]{1,0:T(2,128)S(1)} %bitcast.8, s32[1,32]{1,0:T(1,128)S(1)} %bitcast.9, bf16[128,1024]{1,0:T(8,128)(2,1)} %tok_hbm.1, ...), custom_call_target="tpu_custom_call" | custom-call | tf_op jit(solution)/shard_map/layer/pallas_call | solution.py:341
  117.8 1.0 hand_on.1
Async XLA Ops:
  0.6 0.7 copy-start
  1.3 0.7 copy-start.1
  2.0 0.7 copy-start.2

commit v4 on v3

--- a/solution.py
+++ b/solution.py
@@ -103,9 +103,9 @@
 
 def layer_kernel(
     nz, cap, subs, early,
-    ids_ref, gates_ref, home_ref, tok_hbm, cot_hbm, up_hbm, down_hbm,
+    ids_hbm, gates_hbm, home_hbm, tok_hbm, cot_hbm, up_hbm, down_hbm,
     out_ref, grad_ref, fup_ref, fdn_ref,
-    tok_ref, cot_ref, up_ref, down_ref, stage, send_x, send_y, recv_x, recv_y, ret_x, ret_y,
+    ids_ref, gates_ref, home_ref, tok_ref, cot_ref, up_ref, down_ref, stage, send_x, send_y, recv_x, recv_y, ret_x, ret_y,
     back_x, back_y, tot_up, tot_dn,
     part_up, part_dn, core_up, core_dn, sum_up, sum_dn, pair_up, pair_dn,
     mine_up, mine_dn, one_up, one_dn, ring_up, ring_dn,
@@ -131,17 +131,20 @@
         tell(peer(nz, 1, i)[1])
         tell(peer(nz, -1, i)[1])
 
+    loads = [
+        pltpu.make_async_copy(src, dst, in_sem.at[n])
+        for n, (src, dst) in enumerate(
+            (
+                (tok_hbm, tok_ref), (cot_hbm, cot_ref), (up_hbm, up_ref), (down_hbm, down_ref),
+                (ids_hbm, ids_ref), (gates_hbm, gates_ref), (home_hbm, home_ref),
+            )
+        )
+    ]
+    for n in (4, 6, 0, 5, 1, 2, 3):
+        loads[n].start()
     each(others, tell_both)
     for to in (partner, beside1, beside3):
         tell(to)
-    loads = [
-        pltpu.make_async_copy(src, dst, in_sem.at[n])
-        for n, (src, dst) in enumerate(
-            ((tok_hbm, tok_ref), (cot_hbm, cot_ref), (up_hbm, up_ref), (down_hbm, down_ref))
-        )
-    ]
-    for load in loads:
-        load.start()
 
     def block_copy(n, sign, src, dst):
         def copy(i):
@@ -166,12 +169,15 @@
             device_id=to, device_id_type=MESH,
         )
 
+    loads[4].wait()
+    loads[6].wait()
     first, second = selections(nz, cap, ids_ref[...], home_ref[...])
     loads[0].wait()
     spread(contract(first + second, tok_ref[...], 1, 0), stage, send_x)
     pl.semaphore_wait(barrier, 2 * others + 3)
     each(others, lambda i: give_x(i).start())
     recv_x[0:size, :] = send_x[0:size, :]
+    loads[5].wait()
     loads[1].wait()
     cot = cot_ref[...].astype(f32)
     picked = contract(first, (as_column(gates_ref[0:1, :]) * cot).astype(bf16), 1, 0)
@@ -315,7 +321,7 @@
 VM = pl.BlockSpec(memory_space=pltpu.VMEM)
 HBM = pl.BlockSpec(memory_space=pltpu.HBM)
 SUBS = 4
-LAYER_VMEM, HAND_VMEM = 54150 * 1024, 2**20
+LAYER_VMEM, HAND_VMEM = 48 * 2**20, 2**20
 EARLY = 10
 
 
@@ -341,9 +347,12 @@
     made = pl.pallas_call(
         functools.partial(layer_kernel, nz, cap, SUBS, early),
         out_shape=results,
-        in_specs=[VM] * 3 + [HBM] * 4,
+        in_specs=[HBM] * 7,
         out_specs=(VM,) * 4,
         scratch_shapes=[
+            pltpu.VMEM((2, tok_count), i32),
+            pltpu.VMEM((2, tok_count), f32),
+            pltpu.VMEM((1, experts), i32),
             pltpu.VMEM((tok_count, width), bf16),
             pltpu.VMEM((tok_count, width), bf16),
             pltpu.VMEM((width, hidden), bf16),
@@ -353,7 +362,7 @@
         + [pltpu.VMEM((flat, LANES), bf16)] * 8
         + both() + both(ny, 2) + both(ny) + both(ny) + both(2) + both(2) + both() + both(half)
         + [
-            dma((4,)), dma((4, experts)), dma((4, experts)), dma((8,)), dma((8,)),
+            dma((7,)), dma((4, experts)), dma((4, experts)), dma((8,)), dma((8,)),
             dma((2, half, SUBS)), dma((2, half, SUBS)),
         ],
         compiler_params=pltpu.CompilerParams(
@@ -361,8 +370,13 @@
         ),
         name="layer",
     )(
-        expert_ids.T, gates.T, expert_home.reshape(1, experts), tokens, cotangent,
-        up_weight.reshape(width, hidden), down_weight.reshape(hidden, width),
+        *(
+            pltpu.with_memory_space_constraint(array, pltpu.HBM)
+            for array in (
+                expert_ids.T, gates.T, expert_home.reshape(1, experts), tokens, cotangent,
+                up_weight.reshape(width, hidden), down_weight.reshape(hidden, width),
+            )
+        )
     )
     layer_out, grad_tokens, fup, fdn = pl.pallas_call(
         hand_on_kernel,

time: 119 us -> 117 us (0.983)
  local copies, waits for them, and re-layouts: 2.01 us -> 0 us
    unnamed x6 -> x0, local copies, waits for them, and re-layouts: 2.01 us -> none
where the time goes in v4:
time: 117 us
  Pallas kernels  116 us (99%)
    pallas_call x1, Pallas kernels, local(): pl.pallas_call(functools.partial(layer_kernel, nz, cap, SUBS, early), out...  115 us

profile of v4, /device:TPU:1, one launch (start us, length us, event | category | flops | bytes accessed | tf_op | source)
XLA Modules:
  0.0 116.7 jit_solution(4960468035784906312)
XLA Ops:
  0.6 115.1 %layer.1 = (bf16[128,1024]{1,0:T(8,128)(2,1)S(1)}, bf16[128,1024]{1,0:T(8,128)(2,1)S(1)}, bf16[128,768]{1,0:T(8,128)(2,1)S(1)}, bf16[768,128]{1,0:T(8,128)(2,1)S(1)}) custom-call(s32[2,128]{1,0:T(2,128)} %bitcast.9, f32[2,128]{1,0:T(2,128)} %bitcast.10, s32[1,32]{1,0:T(1,128)} %bitcast.11, bf16[128,1024]{1,0:T(8,128)(2,1)} %tok_hbm.1, ...), custom_call_target="tpu_custom_call" | custom-call | tf_op jit(solution)/shard_map/layer/pallas_call | solution.py:347
  115.7 1.0 hand_on.1

commit v5 on v4

--- a/solution.py
+++ b/solution.py
@@ -19,7 +19,7 @@
 
 
 def z_shift(o, core, w):
-    return o - w * ((o + core) // (w // 2 + 1))
+    return o - w * lax.div(o + core + (w // 2 - 1), w)
 
 
 def contract(a, b, da, db):
@@ -75,17 +75,18 @@
 
 
 def far_order(i, w):
-    k = i // NX
-    o = w // 2 + k // 2 - (k % 2) * (2 * (k // 2) + 1)
-    return o, NX - 1 - i % NX
+    k = lax.div(i, NX)
+    twos = lax.div(k, 2)
+    o = w // 2 + twos - lax.rem(k, 2) * (2 * twos + 1)
+    return o, NX - 1 - lax.rem(i, NX)
 
 
 def peer(nz, sign, i):
     dp, z, x = place()
     w = nz // 2
     o, xo = far_order(i, w)
-    to_z = (z + nz + sign * z_shift(o, dp % 2, w)) % nz
-    to_x = (x + NX + sign * xo) % NX
+    to_z = lax.rem(z + nz + sign * z_shift(o, dp % 2, w), nz)
+    to_x = lax.rem(x + NX + sign * xo, NX)
     return o * NX + xo, (dp, to_z * NX + to_x)
 
 
@@ -152,11 +153,26 @@
             at = pl.ds(pl.multiple_of(b * size, size), size)
             return pltpu.make_async_remote_copy(
                 src_ref=src.at[at, :], dst_ref=dst.at[at, :],
-                send_sem=block_send.at[n, b], recv_sem=block_recv.at[n, b],
+                send_sem=block_send.at[n], recv_sem=block_recv.at[n],
                 device_id=to, device_id_type=MESH,
             )
 
         return copy
+
+    def all_blocks(n, src, dst):
+        rest = pl.ds(size, others * size)
+        return pltpu.make_async_remote_copy(
+            src_ref=src.at[rest, :], dst_ref=dst.at[rest, :],
+            send_sem=block_send.at[n], recv_sem=block_recv.at[n],
+            device_id=partner, device_id_type=MESH,
+        )
+
+    whole = [
+        all_blocks(n, src, dst)
+        for n, (src, dst) in enumerate(
+            ((send_x, recv_x), (send_y, recv_y), (ret_x, back_x), (ret_y, back_y))
+        )
+    ]
 
     give_x = block_copy(0, 1, send_x, recv_x)
     give_y = block_copy(1, 1, send_y, recv_y)
@@ -189,7 +205,7 @@
     loads[2].wait()
     loads[3].wait()
     chunks = up_ref.shape[0] // LANES
-    each(others, lambda i: give_x(i).wait_recv())
+    whole[0].wait_recv()
     in_rows = gather_rows(recv_x[...], stage, chunks)
     pre = contract(in_rows, up_ref[...], 1, 0)
     sig = 1.0 / (1.0 + jnp.exp(-pre))
@@ -200,7 +216,7 @@
     back_x[0:size, :] = ret_x[0:size, :]
     each(early, lambda i: return_x(i).start())
 
-    each(others, lambda i: give_y(i).wait_recv())
+    whole[1].wait_recv()
     each(others, lambda i: return_x(i).start(), early)
     dy = gather_rows(recv_y[...], stage, chunks)
     pre_grad = (contract(dy, down_ref[...], 1, 1) * slope).astype(bf16)
@@ -280,26 +296,27 @@
             hop(d, j, k, k + 1).start()
 
     each(half - 1, forward)
-    each(others, lambda i: return_x(i).wait_recv())
+    whole[2].wait_recv()
     outs = gather_rows(back_x[...], stage, chunks)
     total = as_column(gates_ref[0:1, :]) * contract(first, outs, 0, 0)
     total += as_column(gates_ref[1:2, :]) * contract(second, outs, 0, 0)
     out_ref[...] = total.astype(bf16)
-    each(others, lambda i: return_y(i).wait_recv())
+    whole[3].wait_recv()
     grads = gather_rows(back_y[...], stage, chunks)
     grad_ref[...] = contract(first + second, grads, 0, 0).astype(bf16)
+
+    def drain(k):
+        for d, j in both:
+            hop(d, j, k, k).wait_send()
+
+    for exchange in whole:
+        exchange.wait_send()
+    each(half - 1, drain)
     for d, j in both:
         hop(d, j, half - 1, half - 1).wait_recv()
     fup_ref[...] = add(tot_up[...], ring_up[half - 1])
     fdn_ref[...] = add(tot_dn[...], ring_dn[half - 1])
-
-    def drain(k):
-        for d, j in both:
-            hop(d, j, k, k).wait_send()
-
-    each(half, drain)
-    for moved in (give_x, give_y, return_x, return_y):
-        each(others, lambda i: moved(i).wait_send())
+    drain(half - 1)
 
 
 def hand_on_kernel(*refs):
@@ -362,7 +379,7 @@
         + [pltpu.VMEM((flat, LANES), bf16)] * 8
         + both() + both(ny, 2) + both(ny) + both(ny) + both(2) + both(2) + both() + both(half)
         + [
-            dma((7,)), dma((4, experts)), dma((4, experts)), dma((8,)), dma((8,)),
+            dma((7,)), dma((4,)), dma((4,)), dma((8,)), dma((8,)),
             dma((2, half, SUBS)), dma((2, half, SUBS)),
         ],
         compiler_params=pltpu.CompilerParams(

time: 117 us -> 111 us (0.949)
  Pallas kernels: 116 us -> 110 us
    pallas_call x1, Pallas kernels: 115 us -> 109 us  [local(): pl.pallas_call(functools.partial(layer_kernel, nz, cap, SUBS, early), out...]
where the time goes in v5:
time: 111 us
  Pallas kernels  110 us (99%)
    pallas_call x1, Pallas kernels, local(): pl.pallas_call(functools.partial(layer_kernel, nz, cap, SUBS, early), out...  109 us

profile of v5, /device:TPU:1, one launch (start us, length us, event | category | flops | bytes accessed | tf_op | source)
XLA Modules:
  0.0 110.7 jit_solution(6760449560140775825)
XLA Ops:
  0.6 109.1 %layer.1 = (bf16[128,1024]{1,0:T(8,128)(2,1)S(1)}, bf16[128,1024]{1,0:T(8,128)(2,1)S(1)}, bf16[128,768]{1,0:T(8,128)(2,1)S(1)}, bf16[768,128]{1,0:T(8,128)(2,1)S(1)}) custom-call(s32[2,128]{1,0:T(2,128)} %bitcast.9, f32[2,128]{1,0:T(2,128)} %bitcast.10, s32[1,32]{1,0:T(1,128)} %bitcast.11, bf16[128,1024]{1,0:T(8,128)(2,1)} %tok_hbm.1, ...), custom_call_target="tpu_custom_call" | custom-call | tf_op jit(solution)/shard_map/layer/pallas_call | solution.py:364
  109.8 1.0 hand_on.1
